TPU v7x, 256 devices: a whole 4x4x8 slice. The times are simulated.
256 devices in a mesh: seq: 32 (over x, y, core), tp: 8 (over z).
Axes of the slice: x: 4, y: 4, z: 8, core: 2. Of those that a mesh axis runs over, the one named last changes fastest.
Arguments:
- hidden: bfloat16 [8192, 1024], P('seq'), may hold values from -6 to 6
- norm1_gain: float32 [1024], replicated, may hold values from 0.25 to 1.75
- w_query: bfloat16 [1024, 1024], P(None, 'tp'), may hold values from -3 to 3
- w_key: bfloat16 [1024, 512], P(None, 'tp'), may hold values from -2 to 2
- w_value: bfloat16 [1024, 512], P(None, 'tp'), may hold values from -0.1875 to 0.1875
- w_out: bfloat16 [1024, 1024], P('tp'), may hold values from -0.1875 to 0.1875
- norm2_gain: float32 [1024], replicated, may hold values from 0.25 to 1.75
- w_gate: bfloat16 [32, 1024, 512], P('seq'), may hold values from -0.1875 to 0.1875
- w_up: bfloat16 [32, 1024, 512], P('seq'), may hold values from -0.1875 to 0.1875
- w_down: bfloat16 [32, 512, 1024], P('seq'), may hold values from -0.25 to 0.25
- cache_in: bfloat16 [288, 256, 8, 128], P('seq', None, 'tp'), may hold values from -48 to 48
- cache_len: int32 [4], replicated, may hold values from 0 to 16384, as said below
- block_table: int32 [288], replicated, may hold values from 0 to 287, each once
- routes: int32 [8192, 8], P(('seq', 'tp')), may hold values from 0 to 31, all different within a row; in each aligned block of 32 rows (0 to 31, 32 to 63, ...) at most 12 rows name the same one
- gate_w: float32 [8192, 8], P(('seq', 'tp')), may hold values from 0.05 to 0.35
Outputs:
- hidden_out: bfloat16 [8192, 1024], P(('seq', 'tp'))
- cache_out: bfloat16 [288, 256, 8, 128], P('seq', None, 'tp')
Inputs may be any that keep to these rules, and one draw needn't show every extreme that they name: `cache_len`: some request holds exactly 16384 entries. `block_table`: each pool block appears once; pool block b lies on index b // 9 of seq. `routes`: each row names 8 different experts; among the rows of one device (aligned blocks of 32 rows) no expert is named more than 12 times, a bound that some block reaches.
All inputs are finite; a program needn't handle non-finite values.
Results may differ from a plain program's by a relative error of at most 0.035.
The roundings to bfloat16 on the way count: a program that leaves them out, or rounds other values in their place, can miss the bound.
Values may be sent and summed in bfloat16 or wider, within the bound.
No kernel may reach another device: no remote copies, remote signals or barrier semaphores. Data moves between devices by JAX's collectives and lax.ppermute only.
A program may use at most 128 MiB of HBM per device.

v0:
```python
import functools
import math

import jax
import jax.numpy as jnp
from jax import lax
from jax.experimental import pallas as pl
from jax.experimental.pallas import tpu as pltpu
from jax.sharding import PartitionSpec as P

D = 1024
HD = 64
GROUP = 2
FFN = 512
TOP = 8
STRETCH = 2048
BS = 256
TOK = 256
MAXB = 72
NB = 9
TILES = 8
ROWS = 32
LINES = 24
PACK = 72
NS = 4

EPS = 1e-05
ROPE_BASE = 10000.0
LOW = -1e30
LOG2E = 1.4426950408889634
F32 = jnp.float32
BF16 = jnp.bfloat16

VM = pl.BlockSpec(memory_space=pltpu.VMEM)
SM = pl.BlockSpec(memory_space=pltpu.SMEM)


def rms(x, gain):
    mean_square = jnp.mean(x * x, axis=-1, keepdims=True)
    return (x * lax.rsqrt(mean_square + EPS) * gain).astype(BF16)


def spin(rows, cosine, sine):
    front, back = rows[:32], rows[32:]
    return jnp.concatenate([front * cosine - back * sine, back * cosine + front * sine], axis=0)


def project_kernel(hidden, gain, wq, wk, wv, cosine, sine, q_out, rows_out):
    normed = rms(hidden[...].astype(F32), gain[...])
    q = jnp.dot(normed, wq[...], preferred_element_type=F32)
    nt = (((1,), (1,)), ((), ()))
    kt = lax.dot_general(wk[...], normed, nt, preferred_element_type=F32)
    vt = lax.dot_general(wv[...], normed, nt, preferred_element_type=F32)
    cos, sin = cosine[...], sine[...]
    qt = q.T
    scale = LOG2E / math.sqrt(HD)
    first = (spin(qt[:64], cos, sin) * scale).astype(BF16)
    second = (spin(qt[64:], cos, sin) * scale).astype(BF16)
    for chip in range(16):
        q_out[2 * chip] = first
        q_out[2 * chip + 1] = second
    rows_out[...] = jnp.concatenate([spin(kt, cos, sin), vt], axis=0).T.astype(BF16)


def attend_kernel(meta, q, own, other, new_own, new_other, out, pool, acc, peak, vt, sbuf):
    pool[0:NB] = own[...]
    pool[NB : 2 * NB] = other[...]
    pool[2 * NB] = new_own[...]
    pool[2 * NB + 1] = new_other[...]
    acc[...] = jnp.zeros_like(acc)
    peak[...] = jnp.full_like(peak, LOW / 2)

    def load(j):
        entries = pool[j]
        turned = entries.astype(F32).T
        ones = (lax.broadcasted_iota(jnp.int32, (8, BS), 0) == 0).astype(F32)
        vt[...] = jnp.concatenate([turned[HD:], ones], axis=0).astype(BF16)
        return entries[:, :HD]

    def score(keys, tile, old, mask, slot):
        scores = jnp.dot(keys, q[tile], preferred_element_type=F32)
        if mask is not None:
            scores = jnp.where(mask, scores, LOW)
        sbuf[slot] = scores
        return jnp.maximum(old, jnp.max(scores, axis=0, keepdims=True))

    def absorb(tile, old, new, slot):
        weights = jnp.exp2(sbuf[slot] - new).astype(BF16)
        keep = jnp.exp2(old - new)
        mixed = jnp.dot(vt[...], weights, preferred_element_type=F32)
        acc[tile] = acc[tile] * keep + mixed

    def sweep(keys, request, mask_of):
        olds = peak[request]
        base = request * TILES
        news = []

        def ahead(t):
            news.append(score(keys, base + t, olds[t : t + 1], mask_of(t), t % NS))

        ahead(0)
        ahead(1)
        for t in range(TILES):
            if t + 2 < TILES:
                ahead(t + 2)
            absorb(base + t, olds[t : t + 1], news[t], t % NS)
        peak[request] = jnp.concatenate(news, axis=0)

    def block(j, carry):
        request = meta[0, j]
        seen = meta[1, j]

        @pl.when(seen >= BS)
        def _():
            sweep(load(j), request, lambda t: None)

        @pl.when((seen > 0) & (seen < BS))
        def _():
            mask = lax.broadcasted_iota(jnp.int32, (BS, TOK), 0) < seen
            sweep(load(j), request, lambda t: mask)

        return carry

    lax.fori_loop(0, 2 * NB, block, 0)
    request = meta[3, 0]

    def fresh(k, carry):
        tile = meta[3, 1 + k]
        gap = lax.broadcasted_iota(jnp.int32, (BS, TOK), 0) - lax.broadcasted_iota(
            jnp.int32, (BS, TOK), 1
        )
        sweep(load(2 * NB + k), request, lambda t: gap <= (t - tile) * TOK)
        return carry

    lax.fori_loop(0, 2, fresh, 0)

    for r in range(4):
        peaks = peak[r]
        for t in range(TILES):
            state = acc[r * TILES + t]
            mass = state[HD : HD + 1]
            some = mass > 0.0
            safe = jnp.where(some, mass, 1.0)
            level = jnp.where(some, peaks[t : t + 1] + jnp.log2(safe), LOW)
            high = level.astype(BF16)
            rest = level - high.astype(F32)
            middle = rest.astype(BF16)
            low = (rest - middle.astype(F32)).astype(BF16)
            share = (state[:HD] * (1.0 / safe)).astype(BF16)
            tail = jnp.concatenate(
                [high.astype(F32), middle.astype(F32), low.astype(F32), jnp.zeros((5, TOK), F32)],
                axis=0,
            ).astype(BF16)
            out[r * TILES + t, 0:HD] = share
            out[r * TILES + t, HD:PACK] = tail


def merge_kernel(parts, w_out, out):
    heads = []
    for h in range(GROUP):
        levels = []
        for i in range(16):
            tail = parts[2 * i + h, HD:PACK].astype(F32)
            levels.append(tail[0:1] + tail[1:2] + tail[2:3])
        top = functools.reduce(jnp.maximum, levels)
        total = jnp.zeros((1, TOK), F32)
        mixed = jnp.zeros((HD, TOK), F32)
        for i in range(16):
            share = jnp.exp2(levels[i] - top)
            total = total + share
            mixed = mixed + parts[2 * i + h, 0:HD].astype(F32) * share
        heads.append(mixed / total)
    attention = jnp.concatenate(heads, axis=0).T.astype(BF16)
    out[...] = jnp.dot(attention, w_out[...], preferred_element_type=F32).astype(BF16)


def one_if(cond):
    return jnp.where(cond, 1.0, 0.0).astype(BF16)


def ranks(routes):
    experts = lax.broadcasted_iota(jnp.int32, (32, ROWS), 0)
    member = jnp.zeros((32, ROWS), F32)
    for k in range(TOP):
        member = member + jnp.where(routes[k : k + 1, :] == experts, 1.0, 0.0)
    before = one_if(
        lax.broadcasted_iota(jnp.int32, (ROWS, ROWS), 0)
        < lax.broadcasted_iota(jnp.int32, (ROWS, ROWS), 1)
    )
    rank = jnp.dot(member.astype(BF16), before, preferred_element_type=F32)
    return jnp.where(member > 0.0, rank, -1.0)


def line_slots(width):
    line = lax.broadcasted_iota(jnp.int32, (32 * LINES, width), 0) % LINES
    tail = line - 16
    slot = jnp.where(line < 16, line % 8, 8 + tail % 4)
    half = jnp.where(line < 16, line // 8, tail // 4)
    return slot.astype(F32), half


def line_experts():
    line = lax.broadcasted_iota(jnp.int32, (32 * LINES, 32), 0) // LINES
    return one_if(line == lax.broadcasted_iota(jnp.int32, (32 * LINES, 32), 1))


def dispatch_kernel(parts, hidden, gain, routes, send_out, residual_out):
    total = parts[0].astype(F32)
    for z in range(1, 8):
        total = total + parts[z].astype(F32)
    residual = (hidden[...].astype(F32) + total).astype(BF16)
    residual_out[...] = residual
    normed = rms(residual.astype(F32), gain[...])
    spread = jnp.dot(line_experts(), ranks(routes).astype(BF16), preferred_element_type=F32)
    slot, half = line_slots(ROWS)
    chosen = spread == slot
    send_out[...] = (
        jnp.dot(one_if(chosen & (half == 0)), normed[:, :512], preferred_element_type=F32)
        + jnp.dot(one_if(chosen & (half == 1)), normed[:, 512:], preferred_element_type=F32)
    ).astype(BF16)


def glu(gate, up):
    return (gate * (1.0 / (1.0 + jnp.exp(-gate))) * up).astype(BF16)


def expert_kernel(rows, w_gate, w_up, w_down, out):
    main = jnp.concatenate(
        [rows[:, 0:8, :].reshape(256, 512), rows[:, 8:16, :].reshape(256, 512)], axis=1
    )
    tail = rows[:, 16:24, :].reshape(256, 512)

    def fold(w):
        low = jnp.dot(tail, w[:512, :], preferred_element_type=F32)
        high = jnp.dot(tail, w[512:, :], preferred_element_type=F32)
        return low + pltpu.roll(high, 252, 0)

    inner = glu(
        jnp.dot(main, w_gate[...], preferred_element_type=F32),
        jnp.dot(main, w_up[...], preferred_element_type=F32),
    )
    answer = jnp.dot(inner, w_down[...], preferred_element_type=F32).astype(BF16)
    out[:, 0:8, :] = answer[:, :512].reshape(32, 8, 512)
    out[:, 8:16, :] = answer[:, 512:].reshape(32, 8, 512)
    inner = glu(fold(w_gate), fold(w_up))
    answer = jnp.dot(inner, w_down[...], preferred_element_type=F32)
    early = lax.broadcasted_iota(jnp.int32, (256, 512), 0) % 8 < 4
    mixed = jnp.where(early, answer[:, :512], pltpu.roll(answer[:, 512:], 4, 0))
    out[:, 16:24, :] = mixed.astype(BF16).reshape(32, 8, 512)


def settle_kernel(answers, residual, routes, gate_w, out):
    experts = lax.broadcasted_iota(jnp.int32, (32, ROWS), 0)
    gains = jnp.zeros((32, ROWS), F32)
    for k in range(TOP):
        gains = gains + jnp.where(routes[k : k + 1, :] == experts, gate_w[k : k + 1, :], 0.0)
    high = gains.astype(BF16).astype(F32)
    middle = (gains - high).astype(BF16).astype(F32)
    low = gains - high - middle
    rank = ranks(routes)
    expand = line_experts()
    places = jnp.dot(
        expand, jnp.concatenate([rank, rank, rank], axis=1).astype(BF16), preferred_element_type=F32
    )
    weights = jnp.dot(
        expand, jnp.concatenate([high, middle, low], axis=1).astype(BF16), preferred_element_type=F32
    )
    slot, half = line_slots(3 * ROWS)
    weights = jnp.where(places == slot, weights, 0.0)
    base = residual[...].astype(F32)
    for h in range(2):
        mix = jnp.where(half == h, weights, 0.0).T.astype(BF16)
        sums = jnp.dot(mix, answers[...], preferred_element_type=F32)
        total = sums[:ROWS] + sums[ROWS : 2 * ROWS] + sums[2 * ROWS :]
        columns = slice(512 * h, 512 * h + 512)
        out[:, columns] = (base[:, columns] + total).astype(BF16)


def cache_kernel(core, meta, cache, near, far, out):
    side = core[0]

    def tile_rows(i):
        return jnp.where(i % 2 == side, near[i // 2].astype(F32), far[i // 2].astype(F32))

    lane = lax.broadcasted_iota(jnp.int32, (BS, 2 * BS), 1)
    line = lax.broadcasted_iota(jnp.int32, (BS, 2 * BS), 0)
    place = lax.broadcasted_iota(jnp.int32, (BS, 2 * HD), 0)

    def block(j, carry):
        shift = meta[2, j]
        out[j] = cache[j]

        @pl.when((shift > -BS) & (shift < STRETCH))
        def _():
            base = (shift + BS) // BS - 1
            turn = shift - base * BS
            start = meta[0, j] * TILES
            left = tile_rows(start + jnp.maximum(base, 0))
            right = tile_rows(start + jnp.minimum(base + 1, TILES - 1))
            both = jnp.concatenate([left, right], axis=0).astype(BF16)
            pick = one_if(lane == line + turn)
            fresh = jnp.dot(pick, both, preferred_element_type=F32)
            inside = (place + shift >= 0) & (place + shift < STRETCH)
            out[j] = jnp.where(inside, fresh, cache[j].astype(F32)).astype(BF16)

        return carry

    lax.fori_loop(0, NB, block, 0)


def on_device(
    hidden,
    norm1_gain,
    w_query,
    w_key,
    w_value,
    w_out,
    norm2_gain,
    w_gate,
    w_up,
    w_down,
    cache_in,
    cache_len,
    block_table,
    routes,
    gate_w,
):
    seq = lax.axis_index("seq")
    tp = lax.axis_index("tp")
    sds = jax.ShapeDtypeStruct
    swap = [(i, i ^ 1) for i in range(32)]
    cache = cache_in.reshape(NB, BS, 2 * HD)
    cache_other = lax.ppermute(cache, "seq", swap)

    request = seq // TILES
    filled = jnp.sum(jnp.where(jnp.arange(4, dtype=jnp.int32) == request, cache_len, 0))
    positions = filled + (seq % TILES) * TOK + jnp.arange(TOK, dtype=jnp.int32)
    counter = jnp.arange(HD // 2, dtype=jnp.int32).astype(F32)
    frequency = jnp.exp(counter * (-2.0 * math.log(ROPE_BASE) / HD))
    angles = frequency[:, None] * positions.astype(F32)[None, :]
    cosine, sine = jnp.cos(angles), jnp.sin(angles)

    q_send, new_rows = pl.pallas_call(
        project_kernel,
        out_shape=(sds((32, HD, TOK), BF16), sds((TOK, 2 * HD), BF16)),
        in_specs=[VM] * 7,
        out_specs=(VM, VM),
        name="project",
    )(hidden, norm1_gain[None, :], w_query, w_key.T, w_value.T, cosine, sine)
    queries = lax.all_to_all(q_send, "seq", 0, 0, tiled=True)
    rows_other = lax.ppermute(new_rows, "seq", swap)
    queries, row_send = lax.optimization_barrier((queries, new_rows))
    row_send = jnp.broadcast_to(row_send[None], (16, TOK, 2 * HD))
    same_core = [[2 * chip + c for chip in range(16)] for c in range(2)]
    rows_near = lax.all_to_all(row_send, "seq", 0, 0, tiled=True, axis_index_groups=same_core)

    counts = jnp.arange(2 * NB, dtype=jnp.int32)
    ids = jnp.where(counts < NB, seq * NB + counts, (seq ^ 1) * NB + counts - NB)
    order = jnp.arange(block_table.shape[0], dtype=jnp.int32)
    slot = jnp.sum(jnp.where(block_table[None, :] == ids[:, None], order[None, :], 0), axis=1)
    block_req = slot // MAXB
    pick = block_req[:, None] == jnp.arange(4, dtype=jnp.int32)[None, :]
    block_len = jnp.sum(jnp.where(pick, cache_len[None, :], 0), axis=1)
    block_pos = slot % MAXB * BS
    shift = block_pos - block_len
    own_tile = seq % TILES
    last = jnp.where(
        counts == 0, request, jnp.where(counts == 1, own_tile, own_tile ^ 1)
    )
    meta = jnp.stack([block_req, jnp.clip(-shift, 0, BS), shift, last])

    partial = pl.pallas_call(
        attend_kernel,
        out_shape=sds((32, PACK, TOK), BF16),
        in_specs=[SM] + [VM] * 5,
        out_specs=VM,
        scratch_shapes=[
            pltpu.VMEM((2 * NB + 2, BS, 2 * HD), BF16),
            pltpu.VMEM((32, PACK, TOK), F32),
            pltpu.VMEM((4, TILES, TOK), F32),
            pltpu.VMEM((PACK, BS), BF16),
            pltpu.VMEM((NS, BS, TOK), F32),
        ],
        name="attend",
    )(meta, queries, cache, cache_other, new_rows, rows_other)
    partial, rows_near = lax.optimization_barrier((partial, rows_near))
    parts = lax.all_to_all(partial, "seq", 0, 0, tiled=True)

    projected = pl.pallas_call(
        merge_kernel,
        out_shape=sds((TOK, D), BF16),
        in_specs=[VM, VM],
        out_specs=VM,
        name="merge",
    )(parts, w_out)
    shares = lax.all_to_all(projected.reshape(8, ROWS, D), "tp", 0, 0, tiled=True)

    own_hidden = lax.dynamic_slice_in_dim(hidden, tp * ROWS, ROWS, 0)
    routes_t, gate_t = routes.T, gate_w.T
    send, residual = pl.pallas_call(
        dispatch_kernel,
        out_shape=(sds((32 * LINES, 512), BF16), sds((ROWS, D), BF16)),
        in_specs=[VM] * 4,
        out_specs=(VM, VM),
        name="dispatch",
    )(shares, own_hidden, norm2_gain[None, :], routes_t)
    incoming = lax.all_to_all(send.reshape(32, LINES, 512), "seq", 0, 0, tiled=True)

    answer = pl.pallas_call(
        expert_kernel,
        out_shape=sds((32, LINES, 512), BF16),
        in_specs=[VM] * 4,
        out_specs=VM,
        name="experts",
    )(incoming, w_gate[0], w_up[0], w_down[0])
    returned = lax.all_to_all(answer, "seq", 0, 0, tiled=True)

    hidden_out = pl.pallas_call(
        settle_kernel,
        out_shape=sds((ROWS, D), BF16),
        in_specs=[VM] * 4,
        out_specs=VM,
        name="settle",
    )(returned.reshape(32 * LINES, 512), residual, routes_t, gate_t)

    rows_far = lax.ppermute(rows_near, "seq", swap)
    core = (seq & 1)[None]
    cache_out = pl.pallas_call(
        cache_kernel,
        out_shape=sds((NB, BS, 2 * HD), BF16),
        in_specs=[SM, SM, VM, VM, VM],
        out_specs=VM,
        name="cache",
    )(core, meta, cache, rows_near, rows_far)
    return (hidden_out, cache_out.reshape(NB, BS, 1, 2 * HD))


def solution(mesh):
    placed = (
        P("seq", None),
        P(),
        P(None, "tp"),
        P(None, "tp"),
        P(None, "tp"),
        P("tp", None),
        P(),
        P("seq", None, None),
        P("seq", None, None),
        P("seq", None, None),
        P("seq", None, "tp", None),
        P(),
        P(),
        P(("seq", "tp"), None),
        P(("seq", "tp"), None),
    )
    return jax.shard_map(
        on_device,
        mesh=mesh,
        in_specs=placed,
        out_specs=(P(("seq", "tp"), None), P("seq", None, "tp", None)),
        check_vma=False,
    )
```

profile of v0, /device:TPU:1, one launch (start us, length us, event | category | flops | bytes accessed | tf_op | source)
XLA Modules:
  0.0 164.5 jit_solution(15004588489306115156)
XLA Ops:
  0.7 1.3 fusion.3
  2.6 0.8 multiply_sine_fusion
  3.5 2.9 %project.1 = (bf16[32,64,256]{2,1,0:T(8,128)(2,1)}, bf16[256,128]{1,0:T(8,128)(2,1)}) custom-call(bf16[256,1024]{1,0:T(8,128)(2,1)} %hidden.1, f32[1,1024]{1,0:T(1,128)} %bitcast.44, bf16[1024,128]{1,0:T(8,128)(2,1)} %wq.1, bf16[64,1024]{1,0:T(8,128)(2,1)} %bitcast.40, bf16[64,1024]{1,0:T(8,128)(2,1)} %bitcast.41, f32[32,256]{1,0:T(8,128)} %get-tuple-element.27.cosine, ...), custom_call_target="tpu_custom_call" | custom-call | tf_op jit(solution)/shard_map/project/pallas_call | solution.py:343
  6.4 8.7 %all-to-all-start = ((bf16[32,64,256]{2,1,0:T(8,128)(2,1)}), bf16[32,64,256]{2,1,0:T(8,128)(2,1)S(1)}, u32[]{:S(2)}, u32[]{:S(2)}) async-start(bf16[32,64,256]{2,1,0:T(8,128)(2,1)} %get-tuple-element.10), calls=%async_computation | async-start | bytes 2097152 | tf_op jit(solution)/shard_map/all_to_all | solution.py:350
  15.1 0.3 collective-permute-start
  15.4 0.3 collective-permute-start.1
  15.9 16.1 %all-to-all-done.q = bf16[32,64,256]{2,1,0:T(8,128)(2,1)S(1)} async-done(((bf16[32,64,256]{2,1,0:T(8,128)(2,1)}), bf16[32,64,256]{2,1,0:T(8,128)(2,1)S(1)}, u32[]{:S(2)}, u32[]{:S(2)}) %all-to-all-start) | async-done | bytes 1048608 | tf_op jit(solution)/shard_map/all_to_all | solution.py:350
  32.0 1.3 broadcast_in_dim.72
  33.3 3.8 %all-to-all-start.1 = ((bf16[16,256,128]{2,1,0:T(8,128)(2,1)}), bf16[16,256,128]{2,1,0:T(8,128)(2,1)S(1)}, u32[]{:S(2)}, u32[]{:S(2)}) async-start(bf16[16,256,128]{2,1,0:T(8,128)(2,1)} %broadcast_in_dim.72), calls=%async_computation.1 | async-start | bytes 2097152 | tf_op jit(solution)/shard_map/all_to_all | solution.py:355
  37.3 0.6 pad_add_fusion.meta
  37.9 0.6 copy-done.9
  38.5 0.8 copy-done.7
  39.3 9.9 %attend.1 = bf16[32,72,256]{2,1,0:T(8,128)(2,1)} custom-call(s32[4,18]{1,0:T(4,128)} %pad_add_fusion.meta, bf16[32,64,256]{2,1,0:T(8,128)(2,1)} %copy-done.1, bf16[9,256,128]{2,1,0:T(8,128)(2,1)} %bitcast.31, bf16[9,256,128]{2,1,0:T(8,128)(2,1)} %copy-done.7, bf16[256,128]{1,0:T(8,128)(2,1)} %get-tuple-element.13.new_own, bf16[256,128]{1,0:T(8,128)(2,1)} %copy-done.9), custom_call_target="tpu_custom_call" | custom-call | tf_op jit(solution)/shard_map/attend/pallas_call | solution.py:372
  49.2 4.8 %all-to-all-done.1.near = bf16[16,256,128]{2,1,0:T(8,128)(2,1)S(1)} async-done(((bf16[16,256,128]{2,1,0:T(8,128)(2,1)}), bf16[16,256,128]{2,1,0:T(8,128)(2,1)S(1)}, u32[]{:S(2)}, u32[]{:S(2)}) %all-to-all-start.1) | async-done | bytes 1048608 | tf_op jit(solution)/shard_map/all_to_all | solution.py:355
  54.0 30.9 %all_to_all.30.parts = bf16[32,72,256]{2,1,0:T(8,128)(2,1)} all-to-all(bf16[32,72,256]{2,1,0:T(8,128)(2,1)} %attend.1), channel_id=1, replica_groups=mesh['seq'=32,'tp'=8] {'seq'}, dimensions={0} | all-to-all | bytes 2359296 | tf_op jit(solution)/shard_map/all_to_all | solution.py:387
  84.9 2.7 %merge.1 = bf16[256,1024]{1,0:T(8,128)(2,1)} custom-call(bf16[32,72,256]{2,1,0:T(8,128)(2,1)} %all_to_all.30.parts, bf16[128,1024]{1,0:T(8,128)(2,1)} %w_out.1), custom_call_target="tpu_custom_call" | custom-call | tf_op jit(solution)/shard_map/merge/pallas_call | solution.py:389
  87.6 8.2 %all-to-all-start.3 = ((bf16[8,32,1024]{2,1,0:T(8,128)(2,1)}), bf16[8,32,1024]{2,1,0:T(8,128)(2,1)S(1)}, u32[]{:S(2)}, u32[]{:S(2)}) async-start(bf16[8,32,1024]{2,1,0:T(8,128)(2,1)} %bitcast.34), calls=%async_computation.3 | async-start | bytes 1048576 | tf_op jit(solution)/shard_map/all_to_all | solution.py:396
  95.8 1.5 constant_dynamic-slice_fusion.hidden
  97.3 16.5 %all-to-all-done.3.parts = bf16[8,32,1024]{2,1,0:T(8,128)(2,1)S(1)} async-done(((bf16[8,32,1024]{2,1,0:T(8,128)(2,1)}), bf16[8,32,1024]{2,1,0:T(8,128)(2,1)S(1)}, u32[]{:S(2)}, u32[]{:S(2)}) %all-to-all-start.3) | async-done | bytes 524320 | tf_op jit(solution)/shard_map/all_to_all | solution.py:396
  113.7 0.8 copy-done.5
  114.5 3.6 %dispatch.1 = (bf16[768,512]{1,0:T(8,128)(2,1)}, bf16[32,1024]{1,0:T(8,128)(2,1)}) custom-call(bf16[8,32,1024]{2,1,0:T(8,128)(2,1)} %copy-done.5, bf16[32,1024]{1,0:T(8,128)(2,1)} %constant_dynamic-slice_fusion.hidden, f32[1,1024]{1,0:T(1,128)} %bitcast.45, s32[8,32]{1,0:T(8,128)} %bitcast.42), custom_call_target="tpu_custom_call" | custom-call | tf_op jit(solution)/shard_map/dispatch/pallas_call | solution.py:400
  118.1 4.0 %all-to-all-start.4 = ((bf16[32,24,512]{2,1,0:T(8,128)(2,1)}), bf16[32,24,512]{2,1,0:T(8,128)(2,1)S(1)}, u32[]{:S(2)}, u32[]{:S(2)}) async-start(bf16[32,24,512]{2,1,0:T(8,128)(2,1)} %bitcast.38), calls=%async_computation.4 | async-start | bytes 1572864 | tf_op jit(solution)/shard_map/all_to_all | solution.py:407
  122.2 0.4 collective-permute-start.2
  122.6 13.9 %all-to-all-done.4.rows = bf16[32,24,512]{2,1,0:T(8,128)(2,1)S(1)} async-done(((bf16[32,24,512]{2,1,0:T(8,128)(2,1)}), bf16[32,24,512]{2,1,0:T(8,128)(2,1)S(1)}, u32[]{:S(2)}, u32[]{:S(2)}) %all-to-all-start.4) | async-done | bytes 786464 | tf_op jit(solution)/shard_map/all_to_all | solution.py:407
  136.5 0.9 copy-done.2
  137.4 5.0 %experts.1 = bf16[32,24,512]{2,1,0:T(8,128)(2,1)} custom-call(bf16[32,24,512]{2,1,0:T(8,128)(2,1)} %copy-done.2, bf16[1024,512]{1,0:T(8,128)(2,1)} %bitcast.35, bf16[1024,512]{1,0:T(8,128)(2,1)} %bitcast.36, bf16[512,1024]{1,0:T(8,128)(2,1)} %bitcast.37), custom_call_target="tpu_custom_call" | custom-call | tf_op jit(solution)/shard_map/experts/pallas_call | solution.py:409
  142.4 3.8 %all-to-all-start.5 = ((bf16[32,24,512]{2,1,0:T(8,128)(2,1)}), bf16[32,24,512]{2,1,0:T(8,128)(2,1)S(1)}, u32[]{:S(2)}, u32[]{:S(2)}) async-start(bf16[32,24,512]{2,1,0:T(8,128)(2,1)} %experts.1), calls=%async_computation.5 | async-start | bytes 1572864 | tf_op jit(solution)/shard_map/all_to_all | solution.py:416
  146.1 1.0 copy-done.6
  147.1 3.2 %cache.1 = bf16[9,256,128]{2,1,0:T(8,128)(2,1)} custom-call(s32[1]{0:T(128)} %bitcast.17.core, s32[4,18]{1,0:T(4,128)} %pad_add_fusion.meta, bf16[9,256,128]{2,1,0:T(8,128)(2,1)} %bitcast.32, bf16[16,256,128]{2,1,0:T(8,128)(2,1)} %copy-done, bf16[16,256,128]{2,1,0:T(8,128)(2,1)} %copy-done.6), custom_call_target="tpu_custom_call" | custom-call | tf_op jit(solution)/shard_map/cache/pallas_call | solution.py:428
  150.3 10.0 %all-to-all-done.5 = bf16[32,24,512]{2,1,0:T(8,128)(2,1)S(1)} async-done(((bf16[32,24,512]{2,1,0:T(8,128)(2,1)}), bf16[32,24,512]{2,1,0:T(8,128)(2,1)S(1)}, u32[]{:S(2)}, u32[]{:S(2)}) %all-to-all-start.5) | async-done | bytes 786464 | tf_op jit(solution)/shard_map/all_to_all | solution.py:416
  160.3 0.9 copy-done.3
  161.2 3.2 %settle.1 = bf16[32,1024]{1,0:T(8,128)(2,1)} custom-call(bf16[768,512]{1,0:T(8,128)(2,1)} %bitcast.30, bf16[32,1024]{1,0:T(8,128)(2,1)} %get-tuple-element.16.residual, s32[8,32]{1,0:T(8,128)} %bitcast.43, f32[8,32]{1,0:T(8,128)} %bitcast.46), custom_call_target="tpu_custom_call" | custom-call | tf_op jit(solution)/shard_map/settle/pallas_call | solution.py:418
  (30 shorter events, 0.4 us)
Async XLA Ops:
  6.4 8.8 %copy-start.4 = (bf16[9,256,1,128]{3,1,2,0:T(8,128)(2,1)S(1)}, bf16[9,256,1,128]{3,1,2,0:T(8,128)(2,1)}, u32[]{:S(2)}) copy-start(bf16[9,256,1,128]{3,1,2,0:T(8,128)(2,1)} %param.25) | copy-start | bytes 1769476
  6.4 9.1 %copy-start.8 = (bf16[256,128]{1,0:T(8,128)(2,1)S(1)}, bf16[256,128]{1,0:T(8,128)(2,1)}, u32[]{:S(2)}) copy-start(bf16[256,128]{1,0:T(8,128)(2,1)} %get-tuple-element.13.new_own) | copy-start | bytes 196612
  6.4 9.4 %copy-start.10 = (s32[288]{0:T(512)S(1)}, s32[288]{0:T(512)}, u32[]{:S(2)}) copy-start(s32[288]{0:T(512)} %param.27) | copy-start | bytes 3460
  6.4 25.6 %all-to-all-start = ((bf16[32,64,256]{2,1,0:T(8,128)(2,1)}), bf16[32,64,256]{2,1,0:T(8,128)(2,1)S(1)}, u32[]{:S(2)}, u32[]{:S(2)}) async-start(bf16[32,64,256]{2,1,0:T(8,128)(2,1)} %get-tuple-element.10), calls=%async_computation | async-start | bytes 2097152 | tf_op jit(solution)/shard_map/all_to_all | solution.py:350
  15.1 22.8 %collective-permute-start = (bf16[9,256,128]{2,1,0:T(8,128)(2,1)S(1)}, bf16[9,256,128]{2,1,0:T(8,128)(2,1)S(1)}, u32[]{:S(2)}, u32[]{:S(2)}) collective-permute-start(bf16[9,256,128]{2,1,0:T(8,128)(2,1)S(1)} %bitcast.33), channel_id=1, source_target_pairs={{0,8},{8,0},{16,24},{24,16},{32,40},{40,32},{48,56},{56,48},{64,72... | collective-permute-start | bytes 1769480 | tf_op jit(solution)/shard_map/ppermute | solution.py:333
  15.4 22.4 %collective-permute-start.1 = (bf16[256,128]{1,0:T(8,128)(2,1)S(1)}, bf16[256,128]{1,0:T(8,128)(2,1)S(1)}, u32[]{:S(2)}, u32[]{:S(2)}) collective-permute-start(bf16[256,128]{1,0:T(8,128)(2,1)S(1)} %copy-done.8), channel_id=1, source_target_pairs={{0,8},{8,0},{16,24},{24,16},{32,40},{40,32},{48,56},{56,48},{64,72... | collective-permute-start | bytes 196616 | tf_op jit(solution)/shard_map/ppermute | solution.py:351
  32.0 1.3 copy-start.1
  33.3 3.9 %copy-start.11 = (s32[4]{0:T(128)S(1)}, s32[4]{0:T(128)}, u32[]{:S(2)}) copy-start(s32[4]{0:T(128)} %param.26) | copy-start | bytes 52
  33.3 20.7 %all-to-all-start.1 = ((bf16[16,256,128]{2,1,0:T(8,128)(2,1)}), bf16[16,256,128]{2,1,0:T(8,128)(2,1)S(1)}, u32[]{:S(2)}, u32[]{:S(2)}) async-start(bf16[16,256,128]{2,1,0:T(8,128)(2,1)} %broadcast_in_dim.72), calls=%async_computation.1 | async-start | bytes 2097152 | tf_op jit(solution)/shard_map/all_to_all | solution.py:355
  37.9 0.6 copy-start.9
  38.5 0.8 copy-start.7
  54.0 68.1 %copy-start = (bf16[16,256,128]{2,1,0:T(8,128)(2,1)}, bf16[16,256,128]{2,1,0:T(8,128)(2,1)S(1)}, u32[]{:S(2)}) copy-start(bf16[16,256,128]{2,1,0:T(8,128)(2,1)S(1)} %all-to-all-done.1.near) | copy-start | bytes 3145732
  87.6 26.2 %all-to-all-start.3 = ((bf16[8,32,1024]{2,1,0:T(8,128)(2,1)}), bf16[8,32,1024]{2,1,0:T(8,128)(2,1)S(1)}, u32[]{:S(2)}, u32[]{:S(2)}) async-start(bf16[8,32,1024]{2,1,0:T(8,128)(2,1)} %bitcast.34), calls=%async_computation.3 | async-start | bytes 1048576 | tf_op jit(solution)/shard_map/all_to_all | solution.py:396
  113.7 0.8 copy-start.5
  118.1 18.4 %all-to-all-start.4 = ((bf16[32,24,512]{2,1,0:T(8,128)(2,1)}), bf16[32,24,512]{2,1,0:T(8,128)(2,1)S(1)}, u32[]{:S(2)}, u32[]{:S(2)}) async-start(bf16[32,24,512]{2,1,0:T(8,128)(2,1)} %bitcast.38), calls=%async_computation.4 | async-start | bytes 1572864 | tf_op jit(solution)/shard_map/all_to_all | solution.py:407
  122.2 24.0 %collective-permute-start.2 = (bf16[16,256,128]{2,1,0:T(8,128)(2,1)S(1)}, bf16[16,256,128]{2,1,0:T(8,128)(2,1)S(1)}, u32[]{:S(2)}, u32[]{:S(2)}) collective-permute-start(bf16[16,256,128]{2,1,0:T(8,128)(2,1)S(1)} %all-to-all-done.1.near), channel_id=1, source_target_pairs={{0,8},{8,0},{16,24},{24,16},{32,40},{40,32},{48,56},{56,48},{64,72... | collective-permute-start | bytes 3145736 | tf_op jit(solution)/shard_map/ppermute | solution.py:426
  136.5 0.9 copy-start.2
  142.4 18.0 %all-to-all-start.5 = ((bf16[32,24,512]{2,1,0:T(8,128)(2,1)}), bf16[32,24,512]{2,1,0:T(8,128)(2,1)S(1)}, u32[]{:S(2)}, u32[]{:S(2)}) async-start(bf16[32,24,512]{2,1,0:T(8,128)(2,1)} %experts.1), calls=%async_computation.5 | async-start | bytes 1572864 | tf_op jit(solution)/shard_map/all_to_all | solution.py:416
  146.1 1.0 copy-start.6
  160.3 0.9 copy-start.3
where the time goes:
time: 163 us; the launch traced here: 164 us
  waiting for transfers between devices  61.4 us (38%)
  blocking collectives  30.9 us (19%)
  Pallas kernels  30.4 us (19%)
  starting transfers between devices  29.6 us (18%)
  local copies, waits for them, and re-layouts  7.73 us (5%)
  other arithmetic  3.04 us (2%)
    all_to_all x1, blocking collectives, on_device(): parts = lax.all_to_all(partial, 'seq', 0, 0, tiled=True)  30.9 us
    all_to_all x1, waiting for transfers between devices, on_device(): lax.all_to_all(projected.reshape(8, ROWS, D), 'tp', 0, 0, tiled=True)  16.5 us
    all_to_all x1, waiting for transfers between devices, on_device(): queries = lax.all_to_all(q_send, 'seq', 0, 0, tiled=True)  16.1 us
    all_to_all x1, waiting for transfers between devices, on_device(): lax.all_to_all(send.reshape(32, LINES, 512), 'seq', 0, 0, tiled=True)  13.9 us
    all_to_all x1, waiting for transfers between devices, on_device(): returned = lax.all_to_all(answer, 'seq', 0, 0, tiled=True)  10 us
    pallas_call x1, Pallas kernels, on_device(): pl.pallas_call(attend_kernel, out_shape=sds((32, PACK, TOK), BF16), in_sp...  9.87 us
    all_to_all x1, starting transfers between devices, on_device(): queries = lax.all_to_all(q_send, 'seq', 0, 0, tiled=True)  8.73 us
    all_to_all x1, starting transfers between devices, on_device(): lax.all_to_all(projected.reshape(8, ROWS, D), 'tp', 0, 0, tiled=True)  8.2 us
  transfers between devices with their start and end apart: 8, of which 5 were waited for; matrix products, arithmetic and copies ran while one was open for 2% of the time, Pallas kernels for 11%

commit v1 on v0

--- a/solution.py
+++ b/solution.py
@@ -33,6 +33,8 @@
 
 VM = pl.BlockSpec(memory_space=pltpu.VMEM)
 SM = pl.BlockSpec(memory_space=pltpu.SMEM)
+ANY = pl.BlockSpec(memory_space=pl.ANY)
+FAR = pl.BlockSpec(memory_space=pltpu.HBM)
 
 
 def rms(x, gain):
@@ -45,13 +47,26 @@
     return jnp.concatenate([front * cosine - back * sine, back * cosine + front * sine], axis=0)
 
 
-def project_kernel(hidden, gain, wq, wk, wv, cosine, sine, q_out, rows_out):
+def turns(filled):
+    seq = lax.axis_index("seq")
+    place = filled[seq // TILES] + (seq % TILES) * TOK
+    places = (place + lax.broadcasted_iota(jnp.int32, (HD // 2, TOK), 1)).astype(F32)
+    counter = lax.broadcasted_iota(jnp.int32, (HD // 2, TOK), 0).astype(F32)
+    angles = places * jnp.exp(counter * (-2.0 * math.log(ROPE_BASE) / HD))
+    cycles = jnp.floor(angles * (0.5 / math.pi) + 0.5)
+    angles = angles - cycles * 6.28125
+    angles = angles - cycles * 0.0019350051879882812
+    angles = angles - cycles * 3.0199159819567387e-07
+    return jnp.cos(angles), jnp.sin(angles)
+
+
+def project_kernel(filled, hidden, gain, wq, wk, wv, q_out, rows_out):
     normed = rms(hidden[...].astype(F32), gain[...])
     q = jnp.dot(normed, wq[...], preferred_element_type=F32)
     nt = (((1,), (1,)), ((), ()))
     kt = lax.dot_general(wk[...], normed, nt, preferred_element_type=F32)
     vt = lax.dot_general(wv[...], normed, nt, preferred_element_type=F32)
-    cos, sin = cosine[...], sine[...]
+    cos, sin = turns(filled)
     qt = q.T
     scale = LOG2E / math.sqrt(HD)
     first = (spin(qt[:64], cos, sin) * scale).astype(BF16)
@@ -62,13 +77,21 @@
     rows_out[...] = jnp.concatenate([spin(kt, cos, sin), vt], axis=0).T.astype(BF16)
 
 
-def attend_kernel(meta, q, own, other, new_own, new_other, out, pool, acc, peak, vt, sbuf):
-    pool[0:NB] = own[...]
-    pool[NB : 2 * NB] = other[...]
-    pool[2 * NB] = new_own[...]
-    pool[2 * NB + 1] = new_other[...]
+def attend_kernel(
+    meta, q, own, other, new_own, new_other, out, pool, acc, peak, vt, sbuf, sems
+):
+    copies = (
+        pltpu.make_async_copy(own, pool.at[0:NB], sems.at[0]),
+        pltpu.make_async_copy(other, pool.at[NB : 2 * NB], sems.at[1]),
+        pltpu.make_async_copy(new_own, pool.at[2 * NB], sems.at[2]),
+        pltpu.make_async_copy(new_other, pool.at[2 * NB + 1], sems.at[3]),
+    )
+    for copy in copies:
+        copy.start()
     acc[...] = jnp.zeros_like(acc)
     peak[...] = jnp.full_like(peak, LOW / 2)
+    for copy in copies:
+        copy.wait()
 
     def load(j):
         entries = pool[j]
@@ -224,7 +247,11 @@
     return (gate * (1.0 / (1.0 + jnp.exp(-gate))) * up).astype(BF16)
 
 
-def expert_kernel(rows, w_gate, w_up, w_down, out):
+def expert_kernel(rows, w_gate, up_far, down_far, out, w_up, w_down, sems):
+    up_copy = pltpu.make_async_copy(up_far.at[0], w_up, sems.at[0])
+    down_copy = pltpu.make_async_copy(down_far.at[0], w_down, sems.at[1])
+    up_copy.start()
+    down_copy.start()
     main = jnp.concatenate(
         [rows[:, 0:8, :].reshape(256, 512), rows[:, 8:16, :].reshape(256, 512)], axis=1
     )
@@ -235,15 +262,16 @@
         high = jnp.dot(tail, w[512:, :], preferred_element_type=F32)
         return low + pltpu.roll(high, 252, 0)
 
-    inner = glu(
-        jnp.dot(main, w_gate[...], preferred_element_type=F32),
-        jnp.dot(main, w_up[...], preferred_element_type=F32),
-    )
+    gate = jnp.dot(main, w_gate[...], preferred_element_type=F32)
+    tail_gate = fold(w_gate)
+    up_copy.wait()
+    inner = glu(gate, jnp.dot(main, w_up[...], preferred_element_type=F32))
+    tail_inner = glu(tail_gate, fold(w_up))
+    down_copy.wait()
     answer = jnp.dot(inner, w_down[...], preferred_element_type=F32).astype(BF16)
     out[:, 0:8, :] = answer[:, :512].reshape(32, 8, 512)
     out[:, 8:16, :] = answer[:, 512:].reshape(32, 8, 512)
-    inner = glu(fold(w_gate), fold(w_up))
-    answer = jnp.dot(inner, w_down[...], preferred_element_type=F32)
+    answer = jnp.dot(tail_inner, w_down[...], preferred_element_type=F32)
     early = lax.broadcasted_iota(jnp.int32, (256, 512), 0) % 8 < 4
     mixed = jnp.where(early, answer[:, :512], pltpu.roll(answer[:, 512:], 4, 0))
     out[:, 16:24, :] = mixed.astype(BF16).reshape(32, 8, 512)
@@ -306,6 +334,14 @@
         return carry
 
     lax.fori_loop(0, NB, block, 0)
+
+
+def near(x):
+    return pltpu.with_memory_space_constraint(x, pltpu.VMEM)
+
+
+def far(x):
+    return pltpu.with_memory_space_constraint(x, pltpu.HBM)
 
 
 def on_device(
@@ -333,26 +369,16 @@
     cache_other = lax.ppermute(cache, "seq", swap)
 
     request = seq // TILES
-    filled = jnp.sum(jnp.where(jnp.arange(4, dtype=jnp.int32) == request, cache_len, 0))
-    positions = filled + (seq % TILES) * TOK + jnp.arange(TOK, dtype=jnp.int32)
-    counter = jnp.arange(HD // 2, dtype=jnp.int32).astype(F32)
-    frequency = jnp.exp(counter * (-2.0 * math.log(ROPE_BASE) / HD))
-    angles = frequency[:, None] * positions.astype(F32)[None, :]
-    cosine, sine = jnp.cos(angles), jnp.sin(angles)
-
     q_send, new_rows = pl.pallas_call(
         project_kernel,
         out_shape=(sds((32, HD, TOK), BF16), sds((TOK, 2 * HD), BF16)),
-        in_specs=[VM] * 7,
+        in_specs=[SM] + [VM] * 5,
         out_specs=(VM, VM),
+        compiler_params=pltpu.CompilerParams(vmem_limit_bytes=8 << 20),
         name="project",
-    )(hidden, norm1_gain[None, :], w_query, w_key.T, w_value.T, cosine, sine)
+    )(cache_len, hidden, norm1_gain[None, :], w_query, w_key.T, w_value.T)
     queries = lax.all_to_all(q_send, "seq", 0, 0, tiled=True)
     rows_other = lax.ppermute(new_rows, "seq", swap)
-    queries, row_send = lax.optimization_barrier((queries, new_rows))
-    row_send = jnp.broadcast_to(row_send[None], (16, TOK, 2 * HD))
-    same_core = [[2 * chip + c for chip in range(16)] for c in range(2)]
-    rows_near = lax.all_to_all(row_send, "seq", 0, 0, tiled=True, axis_index_groups=same_core)
 
     counts = jnp.arange(2 * NB, dtype=jnp.int32)
     ids = jnp.where(counts < NB, seq * NB + counts, (seq ^ 1) * NB + counts - NB)
@@ -369,10 +395,17 @@
     )
     meta = jnp.stack([block_req, jnp.clip(-shift, 0, BS), shift, last])
 
+    row_send = jnp.broadcast_to(new_rows[None], (16, TOK, 2 * HD))
+    queries, row_send, meta, cache_other, rows_other = lax.optimization_barrier(
+        (queries, row_send, meta, cache_other, rows_other)
+    )
+    same_core = [[2 * chip + c for chip in range(16)] for c in range(2)]
+    rows_near = lax.all_to_all(row_send, "seq", 0, 0, tiled=True, axis_index_groups=same_core)
+
     partial = pl.pallas_call(
         attend_kernel,
         out_shape=sds((32, PACK, TOK), BF16),
-        in_specs=[SM] + [VM] * 5,
+        in_specs=[SM, VM, FAR, ANY, ANY, ANY],
         out_specs=VM,
         scratch_shapes=[
             pltpu.VMEM((2 * NB + 2, BS, 2 * HD), BF16),
@@ -380,9 +413,11 @@
             pltpu.VMEM((4, TILES, TOK), F32),
             pltpu.VMEM((PACK, BS), BF16),
             pltpu.VMEM((NS, BS, TOK), F32),
+            pltpu.SemaphoreType.DMA((4,)),
         ],
+        compiler_params=pltpu.CompilerParams(vmem_limit_bytes=16 << 20),
         name="attend",
-    )(meta, queries, cache, cache_other, new_rows, rows_other)
+    )(meta, near(queries), far(cache), far(cache_other), new_rows, rows_other)
     partial, rows_near = lax.optimization_barrier((partial, rows_near))
     parts = lax.all_to_all(partial, "seq", 0, 0, tiled=True)
 
@@ -391,6 +426,7 @@
         out_shape=sds((TOK, D), BF16),
         in_specs=[VM, VM],
         out_specs=VM,
+        compiler_params=pltpu.CompilerParams(vmem_limit_bytes=8 << 20),
         name="merge",
     )(parts, w_out)
     shares = lax.all_to_all(projected.reshape(8, ROWS, D), "tp", 0, 0, tiled=True)
@@ -402,17 +438,24 @@
         out_shape=(sds((32 * LINES, 512), BF16), sds((ROWS, D), BF16)),
         in_specs=[VM] * 4,
         out_specs=(VM, VM),
+        compiler_params=pltpu.CompilerParams(vmem_limit_bytes=8 << 20),
         name="dispatch",
-    )(shares, own_hidden, norm2_gain[None, :], routes_t)
+    )(near(shares), own_hidden, norm2_gain[None, :], routes_t)
     incoming = lax.all_to_all(send.reshape(32, LINES, 512), "seq", 0, 0, tiled=True)
 
     answer = pl.pallas_call(
         expert_kernel,
         out_shape=sds((32, LINES, 512), BF16),
-        in_specs=[VM] * 4,
+        in_specs=[VM, VM, FAR, FAR],
         out_specs=VM,
+        scratch_shapes=[
+            pltpu.VMEM((D, FFN), BF16),
+            pltpu.VMEM((FFN, D), BF16),
+            pltpu.SemaphoreType.DMA((2,)),
+        ],
+        compiler_params=pltpu.CompilerParams(vmem_limit_bytes=20 << 20),
         name="experts",
-    )(incoming, w_gate[0], w_up[0], w_down[0])
+    )(near(incoming), near(w_gate[0]), far(w_up), far(w_down))
     returned = lax.all_to_all(answer, "seq", 0, 0, tiled=True)
 
     hidden_out = pl.pallas_call(
@@ -420,6 +463,7 @@
         out_shape=sds((ROWS, D), BF16),
         in_specs=[VM] * 4,
         out_specs=VM,
+        compiler_params=pltpu.CompilerParams(vmem_limit_bytes=8 << 20),
         name="settle",
     )(returned.reshape(32 * LINES, 512), residual, routes_t, gate_t)
 
@@ -430,6 +474,7 @@
         out_shape=sds((NB, BS, 2 * HD), BF16),
         in_specs=[SM, SM, VM, VM, VM],
         out_specs=VM,
+        compiler_params=pltpu.CompilerParams(vmem_limit_bytes=12 << 20),
         name="cache",
     )(core, meta, cache, rows_near, rows_far)
     return (hidden_out, cache_out.reshape(NB, BS, 1, 2 * HD))

time: 163 us -> 155 us (0.951); the launches traced: 164 us -> 155 us
  blocking collectives: 30.9 us -> 26.4 us
  other arithmetic: 3.04 us -> 0.34 us
    pallas_call x1, Pallas kernels: 9.87 us -> 15.1 us  [on_device(): pl.pallas_call(attend_kernel, out_shape=sds((32, PACK, TOK), BF16), in_sp...]
    all_to_all x1, blocking collectives: 30.9 us -> 26.4 us  [on_device(): parts = lax.all_to_all(partial, 'seq', 0, 0, tiled=True)]
    all_to_all x1, waiting for transfers between devices: 4.84 us -> 1.75 us  [on_device(): lax.all_to_all(row_send, 'seq', 0, 0, tiled=True, axis_index_groups=same_...]
    ppermute x1, starting transfers between devices: 0.27 us -> 3.2 us  [on_device(): rows_other = lax.ppermute(new_rows, 'seq', swap)]
    all_to_all x1, starting transfers between devices: 8.73 us -> 5.81 us  [on_device(): queries = lax.all_to_all(q_send, 'seq', 0, 0, tiled=True)]
    pallas_call x1, Pallas kernels: 3.55 us -> 1.58 us  [on_device(): pl.pallas_call(dispatch_kernel, out_shape=(sds((32 * LINES, 512), BF16),...]
    all_to_all x1, waiting for transfers between devices: 10 us -> 11.7 us  [on_device(): returned = lax.all_to_all(answer, 'seq', 0, 0, tiled=True)]
    unnamed x24 -> x32, local copies, waits for them, and re-layouts: 4.97 us -> 6.05 us
  transfers between devices with their start and end apart: 8 -> 8, of which waited for: 5 -> 5; matrix products, arithmetic and copies ran while one was open for 2% -> 1% of each run, Pallas kernels for 11% -> 14%
where the time goes in v1:
time: 155 us
  waiting for transfers between devices  60.9 us (39%)
  starting transfers between devices  29.3 us (19%)
  Pallas kernels  28.8 us (19%)
  blocking collectives  26.4 us (17%)
  local copies, waits for them, and re-layouts  8.2 us (5%)
    all_to_all x1, blocking collectives, on_device(): parts = lax.all_to_all(partial, 'seq', 0, 0, tiled=True)  26.4 us
    all_to_all x1, waiting for transfers between devices, on_device(): lax.all_to_all(projected.reshape(8, ROWS, D), 'tp', 0, 0, tiled=True)  17 us
    all_to_all x1, waiting for transfers between devices, on_device(): queries = lax.all_to_all(q_send, 'seq', 0, 0, tiled=True)  16.5 us
    pallas_call x1, Pallas kernels, on_device(): pl.pallas_call(attend_kernel, out_shape=sds((32, PACK, TOK), BF16), in_sp...  15.1 us
    all_to_all x1, waiting for transfers between devices, on_device(): lax.all_to_all(send.reshape(32, LINES, 512), 'seq', 0, 0, tiled=True)  13.9 us
    all_to_all x1, waiting for transfers between devices, on_device(): returned = lax.all_to_all(answer, 'seq', 0, 0, tiled=True)  11.7 us
    all_to_all x1, starting transfers between devices, on_device(): lax.all_to_all(projected.reshape(8, ROWS, D), 'tp', 0, 0, tiled=True)  8.17 us
    unnamed x32, local copies, waits for them, and re-layouts  6.05 us
  transfers between devices with their start and end apart: 8, of which 5 were waited for; matrix products, arithmetic and copies ran while one was open for 1% of the time, Pallas kernels for 14%

profile of v1, /device:TPU:1, one launch (start us, length us, event | category | flops | bytes accessed | tf_op | source)
XLA Modules:
  0.0 154.8 jit_solution(16933786209622917591)
XLA Ops:
  0.6 1.0 copy-done.3
  1.7 0.9 copy-done.5
  2.6 0.9 copy-done.6
  3.5 0.9 copy-done.7
  4.4 0.7 copy-done.9
  5.1 0.7 copy-done.12
  5.8 2.3 %project.1 = (bf16[32,64,256]{2,1,0:T(8,128)(2,1)}, bf16[256,128]{1,0:T(8,128)(2,1)S(1)}) custom-call(s32[4]{0:T(128)S(1)} %copy-done.12, bf16[256,1024]{1,0:T(8,128)(2,1)S(1)} %copy-done.3, f32[1,1024]{1,0:T(1,128)S(1)} %bitcast.38, bf16[1024,128]{1,0:T(8,128)(2,1)S(1)} %copy-done.5, bf16[64,1024]{1,0:T(8,128)(2,1)S(1)} %bitcast.34, ...), custom_call_target="tpu_custom_call" | custom-call | tf_op jit(solution)/shard_map/project/pallas_call | solution.py:372
  8.1 3.2 %collective-permute-start.1 = (bf16[256,128]{1,0:T(8,128)(2,1)S(1)}, bf16[256,128]{1,0:T(8,128)(2,1)S(1)}, u32[]{:S(2)}, u32[]{:S(2)}) collective-permute-start(bf16[256,128]{1,0:T(8,128)(2,1)S(1)} %get-tuple-element.14.new_own), channel_id=1, source_target_pairs={{0,8},{8,0},{16,24},{24,16},{32,40},{40,32},{48,56},{56,48},{64,72... | collective-permute-start | bytes 196616 | tf_op jit(solution)/shard_map/ppermute | solution.py:381
  11.3 0.1 collective-permute-start
  11.4 5.8 %all-to-all-start = ((bf16[32,64,256]{2,1,0:T(8,128)(2,1)}), bf16[32,64,256]{2,1,0:T(8,128)(2,1)S(1)}, u32[]{:S(2)}, u32[]{:S(2)}) async-start(bf16[32,64,256]{2,1,0:T(8,128)(2,1)} %get-tuple-element.13), calls=%async_computation | async-start | bytes 2097152 | tf_op jit(solution)/shard_map/all_to_all | solution.py:380
  17.3 0.2 select_reduce_fusion
  17.5 0.1 select_reduce_fusion.1
  17.7 16.5 %all-to-all-done.q = bf16[32,64,256]{2,1,0:T(8,128)(2,1)S(1)} async-done(((bf16[32,64,256]{2,1,0:T(8,128)(2,1)}), bf16[32,64,256]{2,1,0:T(8,128)(2,1)S(1)}, u32[]{:S(2)}, u32[]{:S(2)}) %all-to-all-start) | async-done | bytes 1048608 | tf_op jit(solution)/shard_map/all_to_all | solution.py:380
  34.1 1.2 broadcast_in_dim.58
  35.4 3.7 %all-to-all-start.1 = ((bf16[16,256,128]{2,1,0:T(8,128)(2,1)}), bf16[16,256,128]{2,1,0:T(8,128)(2,1)S(1)}, u32[]{:S(2)}, u32[]{:S(2)}) async-start(bf16[16,256,128]{2,1,0:T(8,128)(2,1)} %broadcast_in_dim.58), calls=%async_computation.1 | async-start | bytes 2097152 | tf_op jit(solution)/shard_map/all_to_all | solution.py:403
  39.0 15.1 %attend.1 = bf16[32,72,256]{2,1,0:T(8,128)(2,1)S(1)} custom-call(s32[4,18]{1,0:T(4,128)S(1)} %pad_add_fusion.meta, bf16[32,64,256]{2,1,0:T(8,128)(2,1)S(1)} %all-to-all-done.q, bf16[9,256,128]{2,1,0:T(8,128)(2,1)} %bitcast.30, bf16[9,256,128]{2,1,0:T(8,128)(2,1)} %copy-done.14, bf16[256,128]{1,0:T(8,128)(2,1)S(1)} %get-tuple-element.14.new_own, ...), custom_call_target="tpu_custom_call" | custom-call | tf_op jit(solution)/shard_map/attend/pallas_call | solution.py:405
  54.2 1.8 %all-to-all-done.1.near = bf16[16,256,128]{2,1,0:T(8,128)(2,1)S(1)} async-done(((bf16[16,256,128]{2,1,0:T(8,128)(2,1)}), bf16[16,256,128]{2,1,0:T(8,128)(2,1)S(1)}, u32[]{:S(2)}, u32[]{:S(2)}) %all-to-all-start.1) | async-done | bytes 1048608 | tf_op jit(solution)/shard_map/all_to_all | solution.py:403
  55.9 26.4 %all_to_all.30.parts = bf16[32,72,256]{2,1,0:T(8,128)(2,1)S(1)} all-to-all(bf16[32,72,256]{2,1,0:T(8,128)(2,1)S(1)} %attend.1), channel_id=1, replica_groups=mesh['seq'=32,'tp'=8] {'seq'}, dimensions={0} | all-to-all | bytes 2359296 | tf_op jit(solution)/shard_map/all_to_all | solution.py:422
  82.3 1.4 merge.1
  83.8 8.2 %all-to-all-start.3 = ((bf16[8,32,1024]{2,1,0:T(8,128)(2,1)}), bf16[8,32,1024]{2,1,0:T(8,128)(2,1)S(1)}, u32[]{:S(2)}, u32[]{:S(2)}) async-start(bf16[8,32,1024]{2,1,0:T(8,128)(2,1)} %bitcast.8), calls=%async_computation.3 | async-start | bytes 1048576 | tf_op jit(solution)/shard_map/all_to_all | solution.py:432
  91.9 0.9 constant_dynamic-slice_fusion.hidden
  92.9 17.0 %all-to-all-done.3.parts = bf16[8,32,1024]{2,1,0:T(8,128)(2,1)S(1)} async-done(((bf16[8,32,1024]{2,1,0:T(8,128)(2,1)}), bf16[8,32,1024]{2,1,0:T(8,128)(2,1)S(1)}, u32[]{:S(2)}, u32[]{:S(2)}) %all-to-all-start.3) | async-done | bytes 524320 | tf_op jit(solution)/shard_map/all_to_all | solution.py:432
  109.9 1.6 %dispatch.1 = (bf16[768,512]{1,0:T(8,128)(2,1)S(1)}, bf16[32,1024]{1,0:T(8,128)(2,1)S(1)}) custom-call(bf16[8,32,1024]{2,1,0:T(8,128)(2,1)S(1)} %all-to-all-done.3.parts, bf16[32,1024]{1,0:T(8,128)(2,1)S(1)} %constant_dynamic-slice_fusion.hidden, f32[1,1024]{1,0:T(1,128)S(1)} %bitcast.39, s32[8,32]{1,0:T(8,128)S(1)} %bitcast.36), custom_call_target="tpu_custom_call" | custom-call | tf_op jit(solution)/shard_map/dispatch/pallas_call | solution.py:436
  111.5 0.9 copy-done.2
  112.4 4.1 %all-to-all-start.4 = ((bf16[32,24,512]{2,1,0:T(8,128)(2,1)}), bf16[32,24,512]{2,1,0:T(8,128)(2,1)S(1)}, u32[]{:S(2)}, u32[]{:S(2)}) async-start(bf16[32,24,512]{2,1,0:T(8,128)(2,1)} %bitcast.33), calls=%async_computation.4 | async-start | bytes 1572864 | tf_op jit(solution)/shard_map/all_to_all | solution.py:444
  116.4 0.4 collective-permute-start.2
  116.9 13.9 %all-to-all-done.4.rows = bf16[32,24,512]{2,1,0:T(8,128)(2,1)S(1)} async-done(((bf16[32,24,512]{2,1,0:T(8,128)(2,1)}), bf16[32,24,512]{2,1,0:T(8,128)(2,1)S(1)}, u32[]{:S(2)}, u32[]{:S(2)}) %all-to-all-start.4) | async-done | bytes 786464 | tf_op jit(solution)/shard_map/all_to_all | solution.py:444
  130.8 3.8 %experts.1 = bf16[32,24,512]{2,1,0:T(8,128)(2,1)} custom-call(bf16[32,24,512]{2,1,0:T(8,128)(2,1)S(1)} %all-to-all-done.4.rows, bf16[1024,512]{1,0:T(8,128)(2,1)S(1)} %bitcast.32, bf16[1,1024,512]{2,1,0:T(8,128)(2,1)} %up_far.1, bf16[1,512,1024]{2,1,0:T(8,128)(2,1)} %down_far.1), custom_call_target="tpu_custom_call" | custom-call | tf_op jit(solution)/shard_map/experts/pallas_call | solution.py:446
  134.6 3.9 %all-to-all-start.5 = ((bf16[32,24,512]{2,1,0:T(8,128)(2,1)}), bf16[32,24,512]{2,1,0:T(8,128)(2,1)S(1)}, u32[]{:S(2)}, u32[]{:S(2)}) async-start(bf16[32,24,512]{2,1,0:T(8,128)(2,1)} %experts.1), calls=%async_computation.5 | async-start | bytes 1572864 | tf_op jit(solution)/shard_map/all_to_all | solution.py:459
  138.5 2.4 %cache.1 = bf16[9,256,128]{2,1,0:T(8,128)(2,1)} custom-call(s32[1]{0:T(128)} %bitcast.15.core, s32[4,18]{1,0:T(4,128)S(1)} %pad_add_fusion.meta, bf16[9,256,128]{2,1,0:T(8,128)(2,1)S(1)} %bitcast.31, bf16[16,256,128]{2,1,0:T(8,128)(2,1)S(1)} %all-to-all-done.1.near, bf16[16,256,128]{2,1,0:T(8,128)(2,1)} %collective-permute-done.2.far), custom_call_target="tpu_custom_call" | custom-call | tf_op jit(solution)/shard_map/cache/pallas_call | solution.py:472
  141.0 11.7 %all-to-all-done.5 = bf16[32,24,512]{2,1,0:T(8,128)(2,1)S(1)} async-done(((bf16[32,24,512]{2,1,0:T(8,128)(2,1)}), bf16[32,24,512]{2,1,0:T(8,128)(2,1)S(1)}, u32[]{:S(2)}, u32[]{:S(2)}) %all-to-all-start.5) | async-done | bytes 786464 | tf_op jit(solution)/shard_map/all_to_all | solution.py:459
  152.7 2.1 %settle.1 = bf16[32,1024]{1,0:T(8,128)(2,1)} custom-call(bf16[768,512]{1,0:T(8,128)(2,1)S(1)} %bitcast.28, bf16[32,1024]{1,0:T(8,128)(2,1)S(1)} %get-tuple-element.22.residual, s32[8,32]{1,0:T(8,128)S(1)} %bitcast.37, f32[8,32]{1,0:T(8,128)S(1)} %bitcast.40), custom_call_target="tpu_custom_call" | custom-call | tf_op jit(solution)/shard_map/settle/pallas_call | solution.py:461
  (34 shorter events, 0.1 us)
Async XLA Ops:
  0.6 1.0 copy-start.3
  1.7 0.9 copy-start.5
  2.6 0.9 copy-start.6
  3.5 0.9 copy-start.7
  4.4 0.7 copy-start.9
  5.1 0.7 copy-start.12
  8.1 9.1 %copy-start.15 = (s32[288]{0:T(512)S(1)}, s32[288]{0:T(512)}, u32[]{:S(2)}) copy-start(s32[288]{0:T(512)} %param.27) | copy-start | bytes 3460
  8.1 9.4 %copy-start.13 = (s32[4]{0:T(128)S(1)}, s32[4]{0:T(128)}, u32[]{:S(2)}) copy-start(s32[4]{0:T(128)} %filled.1) | copy-start | bytes 52
  8.1 9.5 %collective-permute-start.1 = (bf16[256,128]{1,0:T(8,128)(2,1)S(1)}, bf16[256,128]{1,0:T(8,128)(2,1)S(1)}, u32[]{:S(2)}, u32[]{:S(2)}) collective-permute-start(bf16[256,128]{1,0:T(8,128)(2,1)S(1)} %get-tuple-element.14.new_own), channel_id=1, source_target_pairs={{0,8},{8,0},{16,24},{24,16},{32,40},{40,32},{48,56},{56,48},{64,72... | collective-permute-start | bytes 196616 | tf_op jit(solution)/shard_map/ppermute | solution.py:381
  11.3 6.3 %collective-permute-start = (bf16[9,256,128]{2,1,0:T(8,128)(2,1)}, bf16[9,256,128]{2,1,0:T(8,128)(2,1)S(1)}, u32[]{:S(2)}, u32[]{:S(2)}) collective-permute-start(bf16[9,256,128]{2,1,0:T(8,128)(2,1)} %bitcast.29), channel_id=1, source_target_pairs={{0,8},{8,0},{16,24},{24,16},{32,40},{40,32},{48,56},{56,48},{64,72... | collective-permute-start | bytes 1769480 | tf_op jit(solution)/shard_map/ppermute | solution.py:369
  11.4 22.7 %all-to-all-start = ((bf16[32,64,256]{2,1,0:T(8,128)(2,1)}), bf16[32,64,256]{2,1,0:T(8,128)(2,1)S(1)}, u32[]{:S(2)}, u32[]{:S(2)}) async-start(bf16[32,64,256]{2,1,0:T(8,128)(2,1)} %get-tuple-element.13), calls=%async_computation | async-start | bytes 2097152 | tf_op jit(solution)/shard_map/all_to_all | solution.py:380
  17.7 17.7 %copy-start.14 = (bf16[9,256,128]{2,1,0:T(8,128)(2,1)}, bf16[9,256,128]{2,1,0:T(8,128)(2,1)S(1)}, u32[]{:S(2)}) copy-start(bf16[9,256,128]{2,1,0:T(8,128)(2,1)S(1)} %collective-permute-done.other) | copy-start | bytes 1769476
  35.4 20.6 %all-to-all-start.1 = ((bf16[16,256,128]{2,1,0:T(8,128)(2,1)}), bf16[16,256,128]{2,1,0:T(8,128)(2,1)S(1)}, u32[]{:S(2)}, u32[]{:S(2)}) async-start(bf16[16,256,128]{2,1,0:T(8,128)(2,1)} %broadcast_in_dim.58), calls=%async_computation.1 | async-start | bytes 2097152 | tf_op jit(solution)/shard_map/all_to_all | solution.py:403
  54.2 28.2 %copy-start.4 = (bf16[128,1024]{1,0:T(8,128)(2,1)S(1)}, bf16[128,1024]{1,0:T(8,128)(2,1)}, u32[]{:S(2)}) copy-start(bf16[128,1024]{1,0:T(8,128)(2,1)} %w_out.1) | copy-start | bytes 786436
  82.3 27.6 %copy-start.8 = (s32[32,8]{0,1:T(8,128)S(1)}, s32[32,8]{0,1:T(8,128)}, u32[]{:S(2)}) copy-start(s32[32,8]{0,1:T(8,128)} %param.28) | copy-start | bytes 3076
  82.3 27.6 %copy-start.10 = (f32[1024]{0:T(1024)S(1)}, f32[1024]{0:T(1024)}, u32[]{:S(2)}) copy-start(f32[1024]{0:T(1024)} %param.21) | copy-start | bytes 12292
  83.8 26.1 %all-to-all-start.3 = ((bf16[8,32,1024]{2,1,0:T(8,128)(2,1)}), bf16[8,32,1024]{2,1,0:T(8,128)(2,1)S(1)}, u32[]{:S(2)}, u32[]{:S(2)}) async-start(bf16[8,32,1024]{2,1,0:T(8,128)(2,1)} %bitcast.8), calls=%async_computation.3 | async-start | bytes 1048576 | tf_op jit(solution)/shard_map/all_to_all | solution.py:432
  91.9 38.8 %copy-start.1 = (bf16[1,1024,512]{2,1,0:T(8,128)(2,1)S(1)}, bf16[1,1024,512]{2,1,0:T(8,128)(2,1)}, u32[]{:S(2)}) copy-start(bf16[1,1024,512]{2,1,0:T(8,128)(2,1)} %param.22) | copy-start | bytes 3145732
  111.5 0.9 copy-start.2
  112.4 18.4 %all-to-all-start.4 = ((bf16[32,24,512]{2,1,0:T(8,128)(2,1)}), bf16[32,24,512]{2,1,0:T(8,128)(2,1)S(1)}, u32[]{:S(2)}, u32[]{:S(2)}) async-start(bf16[32,24,512]{2,1,0:T(8,128)(2,1)} %bitcast.33), calls=%async_computation.4 | async-start | bytes 1572864 | tf_op jit(solution)/shard_map/all_to_all | solution.py:444
  116.4 22.1 %collective-permute-start.2 = (bf16[16,256,128]{2,1,0:T(8,128)(2,1)S(1)}, bf16[16,256,128]{2,1,0:T(8,128)(2,1)}, u32[]{:S(2)}, u32[]{:S(2)}) collective-permute-start(bf16[16,256,128]{2,1,0:T(8,128)(2,1)S(1)} %all-to-all-done.1.near), channel_id=1, source_target_pairs={{0,8},{8,0},{16,24},{24,16},{32,40},{40,32},{48,56},{56,48},{64,72... | collective-permute-start | bytes 3145736 | tf_op jit(solution)/shard_map/ppermute | solution.py:470
  134.6 3.9 %copy-start = (bf16[9,256,1,128]{3,1,2,0:T(8,128)(2,1)S(1)}, bf16[9,256,1,128]{3,1,2,0:T(8,128)(2,1)}, u32[]{:S(2)}) copy-start(bf16[9,256,1,128]{3,1,2,0:T(8,128)(2,1)} %param.25) | copy-start | bytes 1769476
  134.6 18.1 %all-to-all-start.5 = ((bf16[32,24,512]{2,1,0:T(8,128)(2,1)}), bf16[32,24,512]{2,1,0:T(8,128)(2,1)S(1)}, u32[]{:S(2)}, u32[]{:S(2)}) async-start(bf16[32,24,512]{2,1,0:T(8,128)(2,1)} %experts.1), calls=%async_computation.5 | async-start | bytes 1572864 | tf_op jit(solution)/shard_map/all_to_all | solution.py:459
  138.5 14.2 %copy-start.11 = (f32[32,8]{0,1:T(8,128)S(1)}, f32[32,8]{0,1:T(8,128)}, u32[]{:S(2)}) copy-start(f32[32,8]{0,1:T(8,128)} %param.29) | copy-start | bytes 3076
